TPU v7x, 256 devices: a whole 4x4x8 slice. The times are simulated.
256 devices in a mesh: zone: 16 (over x, y), tile: 16 (over z, core).
Axes of the slice: x: 4, y: 4, z: 8, core: 2. Of those that a mesh axis runs over, the one named last changes fastest.
Arguments:
- strips: bfloat16 [12288, 8, 13, 256], P(('zone', 'tile')), may hold values from -6 to 6
- footprint: int32 [12288, 1], P(('zone', 'tile')), may hold values from 0 to 15; in each aligned block of 48 rows (0 to 47, 48 to 95, ...) at most 7 rows name the same one
- row_block: int32 [12288], P(('zone', 'tile')), may hold values from 0 to 7
- date_slot: int32 [12288], P(('zone', 'tile')), may hold values from 0 to 11
- quality: int32 [12288], P(('zone', 'tile')), may hold values from 0 to 3
- date_gain: float32 [12], replicated, may hold values from 0.3 to 3
- reprojection: bfloat16 [256, 128], replicated, may hold values from -0.2 to 0.7
- stem_weight: bfloat16 [13, 128], replicated, may hold values from -1.75 to 1.75
- stem_bias: float32 [128], replicated, may hold values from -3 to 3
- depth_near: bfloat16 [9, 128], replicated, may hold values from -2 to 2
- gain_near: float32 [128], replicated, may hold values from 0.5 to 1.5
- up_near: bfloat16 [128, 512], replicated, may hold values from -0.5 to 0.5
- down_near: bfloat16 [512, 128], replicated, may hold values from -0.25 to 0.25
- depth_far: bfloat16 [9, 128], replicated, may hold values from -2 to 2
- gain_far: float32 [128], replicated, may hold values from 0.5 to 1.5
- up_far: bfloat16 [128, 512], replicated, may hold values from -0.5 to 0.5
- down_far: bfloat16 [512, 128], replicated, may hold values from -0.25 to 0.25
- class_weight: bfloat16 [128, 11], replicated, may hold values from -8 to 8
- class_bias: float32 [11], replicated, may hold values from -4 to 4
Outputs:
- probs: float32 [1024, 11, 2048], P('zone', None, 'tile')
Inputs may be any that keep to these rules, and one draw needn't show every extreme that they name: `footprint`: in the rows of one device no tile is named by more than 7 strips.
All inputs are finite; a program needn't handle non-finite values.
Results may differ from a plain program's by a relative error of at most 0.015.
Values may be sent and summed in bfloat16 or wider, within the bound.
A program may use at most 64 MiB of HBM per device.

v0:
```python
import jax
import jax.numpy as jnp
from jax import lax
from jax.sharding import PartitionSpec as P

TROWS = 64


def padded_2(value, sides, width):
    for axis, dim in sides:
        count, length = (lax.axis_size(axis), value.shape[dim])
        up = [(i, (i + 1) % count) for i in range(count - 1)]
        down = [(j, i) for i, j in up]
        last = lax.slice_in_dim(value, length - width, length, axis=dim)
        leading = lax.slice_in_dim(value, 0, width, axis=dim)
        before = lax.ppermute(last, axis, up)
        after = lax.ppermute(leading, axis, down)
        value = jnp.concatenate([before, value, after], axis=dim)
    return value


def convnext(features, padded, depth, gain, up, down, reach):
    rows = features.shape[0]
    chans = features.shape[1]
    cols = features.shape[2]

    def one_block(index):
        start = index * 8
        window = lax.dynamic_slice_in_dim(padded, start, 8 + 2 * reach, 0)
        current = lax.dynamic_slice_in_dim(features, start, 8, 0)
        total = jnp.zeros((8, chans, cols), jnp.float32)
        for shift_row in range(3):
            for shift_col in range(3):
                tap = depth[shift_row * 3 + shift_col].astype(jnp.float32)[None, :, None]
                piece = window[
                    shift_row * reach : shift_row * reach + 8,
                    :,
                    shift_col * reach : shift_col * reach + cols,
                ]
                total = total + tap * piece.astype(jnp.float32)
        average = jnp.mean(total, axis=1, keepdims=True)
        centred = total - average
        spread = jnp.mean(centred * centred, axis=1, keepdims=True)
        normed = (centred * lax.rsqrt(spread + 1e-05) * gain[None, :, None]).astype(jnp.bfloat16)
        hidden = jax.nn.gelu(
            jnp.einsum("rco,ch->rho", normed, up, preferred_element_type=jnp.float32),
            approximate=True,
        ).astype(jnp.bfloat16)
        update = jnp.einsum("rho,hc->rco", hidden, down, preferred_element_type=jnp.float32)
        return (current.astype(jnp.float32) + update).astype(jnp.bfloat16)

    pieces = lax.map(one_block, jnp.arange(rows // 8, dtype=jnp.int32))
    return pieces.reshape(rows, chans, cols)


def shards(
    strips,
    footprint,
    row_block,
    date_slot,
    quality,
    date_gain,
    reprojection,
    stem_weight,
    stem_bias,
    depth_near,
    gain_near,
    up_near,
    down_near,
    depth_far,
    gain_far,
    up_far,
    down_far,
    class_weight,
    class_bias,
):
    strip_count = strips.shape[0]
    line_count = strips.shape[1]
    band_count = strips.shape[2]
    pixels = strips.shape[3]
    out_pixels = reprojection.shape[1]
    owners = lax.axis_size("tile")
    capacity = max(2, 5 * strip_count // (2 * owners))
    tile_rows = TROWS
    blocks = tile_rows // line_count
    date_count = date_gain.shape[0]
    date_hit = date_slot[:, None] == jnp.arange(date_count, dtype=jnp.int32)[None, :]
    gain_each = jnp.sum(jnp.where(date_hit, date_gain[None, :], 0.0), axis=1)
    strip_weight = (quality.astype(jnp.float32) / 3.0 * gain_each).astype(jnp.bfloat16)
    row_hit = row_block[:, None] == jnp.arange(blocks, dtype=jnp.int32)[None, :]
    placement = jnp.where(row_hit, strip_weight[:, None], jnp.zeros((), jnp.bfloat16))
    target = footprint[:, 0]
    owner_hit = (target[:, None] == jnp.arange(owners, dtype=jnp.int32)[None, :]).astype(jnp.int32)
    earlier = jnp.cumsum(owner_hit, axis=0) - owner_hit
    slot_rank = jnp.sum(earlier * owner_hit, axis=1)
    position = target * capacity + slot_rank
    flattened = strips.reshape(strip_count, line_count * band_count, pixels)
    placed = jnp.zeros((owners * capacity, blocks), jnp.bfloat16).at[position].set(placement)
    placed = placed.reshape(owners, capacity, blocks)
    outgoing = (
        jnp.zeros((owners * capacity, line_count * band_count, pixels), jnp.bfloat16)
        .at[position]
        .set(flattened)
    )
    outgoing = outgoing.reshape(owners, capacity, line_count * band_count, pixels)
    raw_slots = lax.all_to_all(outgoing, "tile", split_axis=0, concat_axis=0, tiled=True)
    slot_weights = lax.all_to_all(placed, "tile", split_axis=0, concat_axis=0, tiled=True)
    mapped = jnp.einsum(
        "nklp,po->nklo", raw_slots, reprojection, preferred_element_type=jnp.float32
    ).astype(jnp.bfloat16)
    numerator = jnp.einsum(
        "nkr,nklo->rlo", slot_weights, mapped, preferred_element_type=jnp.float32
    )
    denominator = jnp.sum(slot_weights.astype(jnp.float32), axis=(0, 1))
    composite = (numerator / jnp.maximum(denominator, 1.0)[:, None, None]).astype(jnp.bfloat16)
    composite = composite.reshape(tile_rows, band_count, out_pixels)
    features0 = (
        jnp.einsum("rbo,bc->rco", composite, stem_weight, preferred_element_type=jnp.float32)
        + stem_bias[None, :, None]
    ).astype(jnp.bfloat16)
    padded_near = padded_2(features0, (("zone", 0), ("tile", 2)), 1)
    features1 = convnext(features0, padded_near, depth_near, gain_near, up_near, down_near, 1)
    padded_far = padded_2(features1, (("zone", 0), ("tile", 2)), 2)
    features2 = convnext(features1, padded_far, depth_far, gain_far, up_far, down_far, 2)
    logits = (
        jnp.einsum("rco,ck->rko", features2, class_weight, preferred_element_type=jnp.float32)
        + class_bias[None, :, None]
    )
    return jax.nn.softmax(logits, axis=1)


def solution(mesh):
    in_specs = (
        P(("zone", "tile"), None, None, None),
        P(("zone", "tile"), None),
        P(("zone", "tile")),
        P(("zone", "tile")),
        P(("zone", "tile")),
        P(),
        P(),
        P(),
        P(),
        P(),
        P(),
        P(),
        P(),
        P(),
        P(),
        P(),
        P(),
        P(),
        P(),
    )
    out_specs = P("zone", None, "tile")
    return jax.shard_map(shards, mesh=mesh, in_specs=in_specs, out_specs=out_specs, check_vma=False)
```

profile of v0, /device:TPU:1, one launch (start us, length us, event | category | flops | bytes accessed | tf_op | source)
XLA Modules:
  0.0 306.6 jit_solution(18224718345200274649)
XLA Ops:
  5.3 10.0 %all-to-all-start = ((bf16[16,7,8]{2,1,0:T(8,128)(2,1)}), bf16[16,7,8]{2,1,0:T(8,128)(2,1)S(1)}, u32[]{:S(2)}, u32[]{:S(2)}) async-start(bf16[16,7,8]{2,1,0:T(8,128)(2,1)} %reshape.235), calls=%async_computation | async-start | bytes 65536 | tf_op jit(solution)/shard_map/all_to_all | solution.py:107
  18.5 3.0 broadcast_in_dim.39
  21.4 7.4 %scatter_fusion = bf16[112,104,256]{2,1,0:T(8,128)(2,1)} fusion(bf16[112,104,256]{2,1,0:T(8,128)(2,1)} %broadcast_in_dim.39, s32[48]{0:T(128)S(1)} %fusion.103, bf16[48,104,256]{2,1,0:T(8,128)(2,1)S(1)} %copy.64), kind=kCustom, calls=%fused_computation.1 | custom fusion | bytes 7667904 | tf_op jit(solution)/shard_map/scatter | solution.py:103
  28.9 7.2 %all-to-all-start.1 = ((bf16[16,7,104,256]{3,2,1,0:T(8,128)(2,1)}), bf16[16,7,104,256]{3,2,1,0:T(8,128)(2,1)}, u32[]{:S(2)}, u32[]{:S(2)}) async-start(bf16[16,7,104,256]{3,2,1,0:T(8,128)(2,1)} %bitcast.195), calls=%async_computation.1 | async-start | bytes 11927552 | tf_op jit(solution)/shard_map/all_to_all | solution.py:106
  36.3 131.4 %all-to-all-done.1 = bf16[16,7,104,256]{3,2,1,0:T(8,128)(2,1)} async-done(((bf16[16,7,104,256]{3,2,1,0:T(8,128)(2,1)}), bf16[16,7,104,256]{3,2,1,0:T(8,128)(2,1)}, u32[]{:S(2)}, u32[]{:S(2)}) %all-to-all-start.1) | async-done | bytes 5963808 | tf_op jit(solution)/shard_map/all_to_all | solution.py:106
  167.6 5.2 %fusion.85 = bf16[8,104,128]{2,0,1:T(8,128)(2,1)S(1)} fusion(bf16[16,7,104,256]{3,2,1,0:T(8,128)(2,1)} %all-to-all-done.1, f32[8]{0:T(128)S(1)} %broadcast_maximum_fusion, bf16[256,128]{1,0:T(8,128)(2,1)S(1)} %copy-done, bf16[16,7,8]{0,2,1:T(8,128)(2,1)S(1)} %copy.66), kind=kOutput, calls=%fused_computation.101 | convolution fusion | flops 788922368 | bytes 6244128 | tf_op jit(solution)/shard_map/nkr,nklo->rlo/dot_general | solution.py:111
  173.8 3.2 %collective-permute-start = (bf16[1,128,128]{1,2,0:T(8,128)(2,1)S(1)}, bf16[1,128,128]{1,2,0:T(8,128)(2,1)S(1)}, u32[]{:S(2)}, u32[]{:S(2)}) collective-permute-start(bf16[1,128,128]{1,2,0:T(8,128)(2,1)S(1)} %get-tuple-element.165), channel_id=1, source_target_pairs={{0,16},{16,32},{32,48},{48,64},{64,80},{80,96},{96,112},{112,128},... | collective-permute-start | bytes 98312 | tf_op jit(solution)/shard_map/ppermute | solution.py:16
  178.3 3.3 %collective-permute-done.1 = bf16[1,128,128]{1,2,0:T(8,128)(2,1)S(1)} collective-permute-done((bf16[1,128,128]{1,2,0:T(8,128)(2,1)S(1)}, bf16[1,128,128]{1,2,0:T(8,128)(2,1)S(1)}, u32[]{:S(2)}, u32[]{:S(2)}) %collective-permute-start.1) | collective-permute-done | bytes 32800 | tf_op jit(solution)/shard_map/ppermute | solution.py:17
  181.7 3.9 %collective-permute-start.2 = (bf16[66,128,1]{1,2,0:T(2,128)(2,1)S(1)}, bf16[66,128,1]{1,2,0:T(2,128)(2,1)S(1)}, u32[]{:S(2)}, u32[]{:S(2)}) collective-permute-start(bf16[66,128,1]{1,2,0:T(2,128)(2,1)S(1)} %get-tuple-element.161), channel_id=1, source_target_pairs={{0,1},{1,2},{2,3},{3,4},{4,5},{5,6},{6,7},{7,8},{8,9},{9,10},{10,1... | collective-permute-start | bytes 50696 | tf_op jit(solution)/shard_map/ppermute | solution.py:16
  187.6 3.3 %collective-permute-done.3 = bf16[66,128,1]{1,2,0:T(2,128)(2,1)S(1)} collective-permute-done((bf16[66,128,1]{1,2,0:T(2,128)(2,1)S(1)}, bf16[66,128,1]{1,2,0:T(2,128)(2,1)S(1)}, u32[]{:S(2)}, u32[]{:S(2)}) %collective-permute-start.3) | collective-permute-done | bytes 16928 | tf_op jit(solution)/shard_map/ppermute | solution.py:17
  190.8 3.6 %pad_maximum_fusion.1 = bf16[66,128,130]{1,2,0:T(8,128)(2,1)S(1)} fusion(bf16[66,128,1]{1,2,0:T(2,128)(2,1)S(1)} %collective-permute-done.3, bf16[1,128,128]{1,2,0:T(8,128)(2,1)S(1)} %collective-permute-done.1, bf16[64,128,128]{1,2,0:T(8,128)(2,1)} %copy-done.1, bf16[1,128,128]{1,2,0:T(8,128)(2,1)S(1)} %collective-permute-done, ...), kind=kLoop, calls=%fused_computation.93 | loop fusion | flops 10982400 | bytes 4392960 | tf_op jit(solution)/shard_map/concatenate | solution.py:18
  196.3 40.9 %while.20 = (s32[]{:T(128)}, bf16[8,8,128,128]{2,3,1,0:T(8,128)(2,1)}, s32[8]{0:T(128)S(1)}, bf16[64,128,128]{1,2,0:T(8,128)(2,1)}, bf16[9,128]{1,0:T(8,128)(2,1...) while((s32[]{:T(128)}, ...), condition=%wide.region_9.10_spmd, body=%wide.region_6.9_spmd.sunk | while | flops 278005888 | bytes 4768304 | solution.py:52
  198.7 2.8 fusion.124
  203.8 2.7 fusion.124
  208.9 2.8 fusion.124
  214.0 2.8 fusion.124
  219.2 2.7 fusion.124
  224.3 2.8 fusion.124
  229.4 2.7 fusion.124
  234.5 2.8 fusion.124
  238.1 3.3 %collective-permute-start.4 = (bf16[2,128,128]{1,2,0:T(8,128)(2,1)S(1)}, bf16[2,128,128]{1,2,0:T(8,128)(2,1)S(1)}, u32[]{:S(2)}, u32[]{:S(2)}) collective-permute-start(bf16[2,128,128]{1,2,0:T(8,128)(2,1)S(1)} %get-tuple-element.163), channel_id=1, source_target_pairs={{0,16},{16,32},{32,48},{48,64},{64,80},{80,96},{96,112},{112,128},... | collective-permute-start | bytes 196616 | tf_op jit(solution)/shard_map/ppermute | solution.py:16
  242.7 3.7 %collective-permute-done.5 = bf16[2,128,128]{1,2,0:T(8,128)(2,1)S(1)} collective-permute-done((bf16[2,128,128]{1,2,0:T(8,128)(2,1)S(1)}, bf16[2,128,128]{1,2,0:T(8,128)(2,1)S(1)}, u32[]{:S(2)}, u32[]{:S(2)}) %collective-permute-start.5) | collective-permute-done | bytes 65568 | tf_op jit(solution)/shard_map/ppermute | solution.py:17
  247.5 3.8 %collective-permute-start.6 = (bf16[68,128,2]{1,2,0:T(2,128)(2,1)S(1)}, bf16[68,128,2]{1,2,0:T(2,128)(2,1)S(1)}, u32[]{:S(2)}, u32[]{:S(2)}) collective-permute-start(bf16[68,128,2]{1,2,0:T(2,128)(2,1)S(1)} %get-tuple-element.159), channel_id=1, source_target_pairs={{0,1},{1,2},{2,3},{3,4},{4,5},{5,6},{6,7},{7,8},{8,9},{9,10},{10,1... | collective-permute-start | bytes 104456 | tf_op jit(solution)/shard_map/ppermute | solution.py:16
  253.4 3.1 %collective-permute-done.7 = bf16[68,128,2]{1,2,0:T(2,128)(2,1)S(1)} collective-permute-done((bf16[68,128,2]{1,2,0:T(2,128)(2,1)S(1)}, bf16[68,128,2]{1,2,0:T(2,128)(2,1)S(1)}, u32[]{:S(2)}, u32[]{:S(2)}) %collective-permute-start.7) | collective-permute-done | bytes 34848 | tf_op jit(solution)/shard_map/ppermute | solution.py:17
  256.5 4.1 %pad_maximum_fusion = bf16[68,128,132]{1,2,0:T(8,128)(2,1)S(1)} fusion(bf16[68,128,2]{1,2,0:T(2,128)(2,1)S(1)} %collective-permute-done.7, bf16[2,128,128]{1,2,0:T(8,128)(2,1)S(1)} %collective-permute-done.5, bf16[64,128,128]{1,2,0:T(8,128)(2,1)} %bitcast.198, bf16[2,128,128]{1,2,0:T(8,128)(2,1)S(1)} %collective-permute-done.4, ...), kind=kLoop, calls=%fused_computation.92 | loop fusion | flops 11489280 | bytes 4595712 | tf_op jit(solution)/shard_map/concatenate | solution.py:18
  262.5 40.9 %while.21 = (s32[]{:T(128)}, bf16[8,8,128,128]{2,3,1,0:T(8,128)(2,1)}, s32[8]{0:T(128)S(1)}, bf16[64,128,128]{1,2,0:T(8,128)(2,1)}, bf16[9,128]{1,0:T(8,128)(2,1...) while((s32[]{:T(128)}, ...), condition=%wide.region_13.14_spmd, body=%wide.region_10.13_spmd.sunk | while | flops 278005888 | bytes 4768304 | solution.py:52
  270.0 2.7 fusion.128
  280.2 2.7 fusion.128
  285.3 2.8 fusion.128
  290.4 2.8 fusion.128
  295.6 2.8 fusion.128
  300.7 2.8 fusion.128
  (162 shorter events, 58.6 us)
Async XLA Ops:
  0.0 167.6 %copy-start = (bf16[256,128]{1,0:T(8,128)(2,1)S(1)}, bf16[256,128]{1,0:T(8,128)(2,1)}, u32[]{:S(2)}) copy-start(bf16[256,128]{1,0:T(8,128)(2,1)} %param.29) | copy-start | bytes 196612
  5.3 23.6 %all-to-all-start = ((bf16[16,7,8]{2,1,0:T(8,128)(2,1)}), bf16[16,7,8]{2,1,0:T(8,128)(2,1)S(1)}, u32[]{:S(2)}, u32[]{:S(2)}) async-start(bf16[16,7,8]{2,1,0:T(8,128)(2,1)} %reshape.235), calls=%async_computation | async-start | bytes 65536 | tf_op jit(solution)/shard_map/all_to_all | solution.py:107
  28.9 138.7 %all-to-all-start.1 = ((bf16[16,7,104,256]{3,2,1,0:T(8,128)(2,1)}), bf16[16,7,104,256]{3,2,1,0:T(8,128)(2,1)}, u32[]{:S(2)}, u32[]{:S(2)}) async-start(bf16[16,7,104,256]{3,2,1,0:T(8,128)(2,1)} %bitcast.195), calls=%async_computation.1 | async-start | bytes 11927552 | tf_op jit(solution)/shard_map/all_to_all | solution.py:106
  36.2 136.7 %copy-start.5 = (bf16[13,128]{1,0:T(8,128)(2,1)S(1)}, bf16[13,128]{1,0:T(8,128)(2,1)}, u32[]{:S(2)}) copy-start(bf16[13,128]{1,0:T(8,128)(2,1)} %param.30) | copy-start | bytes 9988
  36.3 136.7 %copy-start.7 = (f32[128]{0:T(128)S(1)}, f32[128]{0:T(128)}, u32[]{:S(2)}) copy-start(f32[128]{0:T(128)} %param.31) | copy-start | bytes 1540
  173.8 7.9 %copy-start.1 = (bf16[64,128,128]{1,2,0:T(8,128)(2,1)}, bf16[64,128,128]{1,2,0:T(8,128)(2,1)S(1)}, u32[]{:S(2)}) copy-start(bf16[64,128,128]{1,2,0:T(8,128)(2,1)S(1)} %fusion.71) | copy-start | bytes 6291460
  173.8 4.5 %collective-permute-start = (bf16[1,128,128]{1,2,0:T(8,128)(2,1)S(1)}, bf16[1,128,128]{1,2,0:T(8,128)(2,1)S(1)}, u32[]{:S(2)}, u32[]{:S(2)}) collective-permute-start(bf16[1,128,128]{1,2,0:T(8,128)(2,1)S(1)} %get-tuple-element.165), channel_id=1, source_target_pairs={{0,16},{16,32},{32,48},{48,64},{64,80},{80,96},{96,112},{112,128},... | collective-permute-start | bytes 98312 | tf_op jit(solution)/shard_map/ppermute | solution.py:16
  177.0 4.7 %collective-permute-start.1 = (bf16[1,128,128]{1,2,0:T(8,128)(2,1)S(1)}, bf16[1,128,128]{1,2,0:T(8,128)(2,1)S(1)}, u32[]{:S(2)}, u32[]{:S(2)}) collective-permute-start(bf16[1,128,128]{1,2,0:T(8,128)(2,1)S(1)} %get-tuple-element.166), channel_id=1, source_target_pairs={{16,0},{32,16},{48,32},{64,48},{80,64},{96,80},{112,96},{128,112},... | collective-permute-start | bytes 98312 | tf_op jit(solution)/shard_map/ppermute | solution.py:17
  181.7 5.9 %collective-permute-start.2 = (bf16[66,128,1]{1,2,0:T(2,128)(2,1)S(1)}, bf16[66,128,1]{1,2,0:T(2,128)(2,1)S(1)}, u32[]{:S(2)}, u32[]{:S(2)}) collective-permute-start(bf16[66,128,1]{1,2,0:T(2,128)(2,1)S(1)} %get-tuple-element.161), channel_id=1, source_target_pairs={{0,1},{1,2},{2,3},{3,4},{4,5},{5,6},{6,7},{7,8},{8,9},{9,10},{10,1... | collective-permute-start | bytes 50696 | tf_op jit(solution)/shard_map/ppermute | solution.py:16
  185.6 5.2 %collective-permute-start.3 = (bf16[66,128,1]{1,2,0:T(2,128)(2,1)S(1)}, bf16[66,128,1]{1,2,0:T(2,128)(2,1)S(1)}, u32[]{:S(2)}, u32[]{:S(2)}) collective-permute-start(bf16[66,128,1]{1,2,0:T(2,128)(2,1)S(1)} %get-tuple-element.162), channel_id=1, source_target_pairs={{1,0},{2,1},{3,2},{4,3},{5,4},{6,5},{7,6},{8,7},{9,8},{10,9},{11,1... | collective-permute-start | bytes 50696 | tf_op jit(solution)/shard_map/ppermute | solution.py:17
  187.5 8.8 %copy-start.2 = (bf16[9,128]{1,0:T(8,128)(2,1)S(1)}, bf16[9,128]{1,0:T(8,128)(2,1)}, u32[]{:S(2)}) copy-start(bf16[9,128]{1,0:T(8,128)(2,1)} %param.32) | copy-start | bytes 6916
  187.5 8.8 %copy-start.8 = (bf16[128,512]{1,0:T(8,128)(2,1)S(1)}, bf16[128,512]{1,0:T(8,128)(2,1)}, u32[]{:S(2)}) copy-start(bf16[128,512]{1,0:T(8,128)(2,1)} %param.34) | copy-start | bytes 393220
  187.5 8.8 %copy-start.9 = (bf16[512,128]{1,0:T(8,128)(2,1)S(1)}, bf16[512,128]{1,0:T(8,128)(2,1)}, u32[]{:S(2)}) copy-start(bf16[512,128]{1,0:T(8,128)(2,1)} %param.35) | copy-start | bytes 393220
  187.5 8.8 %copy-start.12 = (f32[128]{0:T(128)S(1)}, f32[128]{0:T(128)}, u32[]{:S(2)}) copy-start(f32[128]{0:T(128)} %param.33) | copy-start | bytes 1540
  238.1 4.6 %collective-permute-start.4 = (bf16[2,128,128]{1,2,0:T(8,128)(2,1)S(1)}, bf16[2,128,128]{1,2,0:T(8,128)(2,1)S(1)}, u32[]{:S(2)}, u32[]{:S(2)}) collective-permute-start(bf16[2,128,128]{1,2,0:T(8,128)(2,1)S(1)} %get-tuple-element.163), channel_id=1, source_target_pairs={{0,16},{16,32},{32,48},{48,64},{64,80},{80,96},{96,112},{112,128},... | collective-permute-start | bytes 196616 | tf_op jit(solution)/shard_map/ppermute | solution.py:16
  241.4 5.0 %collective-permute-start.5 = (bf16[2,128,128]{1,2,0:T(8,128)(2,1)S(1)}, bf16[2,128,128]{1,2,0:T(8,128)(2,1)S(1)}, u32[]{:S(2)}, u32[]{:S(2)}) collective-permute-start(bf16[2,128,128]{1,2,0:T(8,128)(2,1)S(1)} %get-tuple-element.164), channel_id=1, source_target_pairs={{16,0},{32,16},{48,32},{64,48},{80,64},{96,80},{112,96},{128,112},... | collective-permute-start | bytes 196616 | tf_op jit(solution)/shard_map/ppermute | solution.py:17
  247.5 5.9 %collective-permute-start.6 = (bf16[68,128,2]{1,2,0:T(2,128)(2,1)S(1)}, bf16[68,128,2]{1,2,0:T(2,128)(2,1)S(1)}, u32[]{:S(2)}, u32[]{:S(2)}) collective-permute-start(bf16[68,128,2]{1,2,0:T(2,128)(2,1)S(1)} %get-tuple-element.159), channel_id=1, source_target_pairs={{0,1},{1,2},{2,3},{3,4},{4,5},{5,6},{6,7},{7,8},{8,9},{9,10},{10,1... | collective-permute-start | bytes 104456 | tf_op jit(solution)/shard_map/ppermute | solution.py:16
  251.2 5.3 %collective-permute-start.7 = (bf16[68,128,2]{1,2,0:T(2,128)(2,1)S(1)}, bf16[68,128,2]{1,2,0:T(2,128)(2,1)S(1)}, u32[]{:S(2)}, u32[]{:S(2)}) collective-permute-start(bf16[68,128,2]{1,2,0:T(2,128)(2,1)S(1)} %get-tuple-element.160), channel_id=1, source_target_pairs={{1,0},{2,1},{3,2},{4,3},{5,4},{6,5},{7,6},{8,7},{9,8},{10,9},{11,1... | collective-permute-start | bytes 104456 | tf_op jit(solution)/shard_map/ppermute | solution.py:17
  253.3 9.1 %copy-start.3 = (bf16[9,128]{1,0:T(8,128)(2,1)S(1)}, bf16[9,128]{1,0:T(8,128)(2,1)}, u32[]{:S(2)}) copy-start(bf16[9,128]{1,0:T(8,128)(2,1)} %param.36) | copy-start | bytes 6916
  253.4 9.1 %copy-start.10 = (bf16[128,512]{1,0:T(8,128)(2,1)S(1)}, bf16[128,512]{1,0:T(8,128)(2,1)}, u32[]{:S(2)}) copy-start(bf16[128,512]{1,0:T(8,128)(2,1)} %param.38) | copy-start | bytes 393220
  253.4 9.1 %copy-start.11 = (bf16[512,128]{1,0:T(8,128)(2,1)S(1)}, bf16[512,128]{1,0:T(8,128)(2,1)}, u32[]{:S(2)}) copy-start(bf16[512,128]{1,0:T(8,128)(2,1)} %param.39) | copy-start | bytes 393220
  253.4 9.1 %copy-start.13 = (f32[128]{0:T(128)S(1)}, f32[128]{0:T(128)}, u32[]{:S(2)}) copy-start(f32[128]{0:T(128)} %param.37) | copy-start | bytes 1540
  262.5 41.0 %copy-start.4 = (bf16[128,11]{0,1:T(8,128)(2,1)S(1)}, bf16[128,11]{0,1:T(8,128)(2,1)}, u32[]{:S(2)}) copy-start(bf16[128,11]{0,1:T(8,128)(2,1)} %param.40) | copy-start | bytes 8452
  262.5 40.9 %copy-start.6 = (f32[11]{0:T(128)S(1)}, f32[11]{0:T(128)}, u32[]{:S(2)}) copy-start(f32[11]{0:T(128)} %param.41) | copy-start | bytes 136
where the time goes:
time: 311 us; the launch traced here: 307 us
  waiting for transfers between devices  145 us (47%)
  matrix products  52.3 us (17%)
  starting transfers between devices  37.9 us (12%)
  other arithmetic  32.5 us (10%)
  local copies, waits for them, and re-layouts  29.1 us (9%)
  loops' own time  9.68 us (3%)
    all_to_all x1, waiting for transfers between devices, shards(): lax.all_to_all(outgoing, 'tile', split_axis=0, concat_axis=0, tiled=True)  131 us
    dot_general x16, matrix products, one_block(): jnp.einsum('rho,hc->rco', hidden, down, preferred_element_type=jnp.float32)  44.1 us
    ppermute x4, starting transfers between devices, padded_2(): before = lax.ppermute(last, axis, up)  14.1 us
    ppermute x4, waiting for transfers between devices, padded_2(): after = lax.ppermute(leading, axis, down)  13.4 us
    reduce_sum x16, other arithmetic, one_block(): average = jnp.mean(total, axis=1, keepdims=True)  12.7 us
    all_to_all x1, starting transfers between devices, shards(): lax.all_to_all(placed, 'tile', split_axis=0, concat_axis=0, tiled=True)  9.98 us
    another operation x2, loops' own time, convnext(): pieces = lax.map(one_block, jnp.arange(rows // 8, dtype=jnp.int32))  9.68 us
    dynamic_slice x16, local copies, waits for them, and re-layouts, convnext(): pieces = lax.map(one_block, jnp.arange(rows // 8, dtype=jnp.int32))  9.2 us
  transfers between devices with their start and end apart: 10, of which 5 were waited for; matrix products, arithmetic and copies ran while one was open for 4% of the time, Pallas kernels for 0%

commit v1 on v0

v1 whole, which is shorter than its diff:
```python
import jax
import jax.numpy as jnp
from jax import lax
from jax.experimental import pallas as pl
from jax.experimental.pallas import tpu as pltpu
from jax.sharding import PartitionSpec as P

F32 = jnp.float32
BF16 = jnp.bfloat16
MESH = pl.DeviceIdType.MESH

N_ZONE = 16
N_TILE = 16
NZ = 8
S = 48
LINES = 8
BANDS = 13
ROWS = 64
RB = 8
CELL = LINES * BANDS
DEN = 16
TILE = DEN + RB * CELL
STEP = 8
CHUNKS = ((0, 224), (224, 208), (432, 208), (640, 208))
HALO = 3
EXT = ROWS + 2 * HALO
MID = ROWS + 4
GROUP1 = 4
GROUP2 = 4


def bin_kernel(fp, rb, ds, q, dg, strips, reproj, out, acc, den):
    step = pl.program_id(0)

    @pl.when(step == 0)
    def _():
        def clear(c, carry):
            acc[c] = jnp.zeros((BANDS, LINES, 128), F32)
            den[c] = jnp.zeros((8, 128), F32)
            return carry

        lax.fori_loop(0, N_TILE * RB, clear, 0)

    p = jnp.dot(strips[...], reproj[...], preferred_element_type=F32)
    for i in range(STEP):
        s = step * STEP + i
        cell = fp[s] * RB + rb[s]
        gain = dg[ds[s]]
        quality = jnp.full((8, 128), q[s], jnp.int32).astype(F32)
        w = (quality / 3.0 * jnp.full((8, 128), gain, F32)).astype(BF16).astype(F32)
        part = p[i * CELL : (i + 1) * CELL, :].reshape(BANDS, LINES, 128)
        acc[cell] = acc[cell] + w[None] * part
        den[cell] = den[cell] + w

    @pl.when(step == S // STEP - 1)
    def _():
        def put(t, carry):
            rows = [den[t * RB + r][0:1, :] for r in range(RB)]
            d = jnp.concatenate(rows, axis=0)
            hi = d.astype(BF16).astype(F32)
            out[t, 0:DEN, :] = jnp.concatenate([hi, d - hi], axis=0).astype(BF16)
            out[t, DEN:TILE, :] = (
                acc[pl.ds(t * RB, RB)].reshape(RB * CELL, 128).astype(BF16)
            )
            return carry

        lax.fori_loop(0, N_TILE, put, 0)


def binned(strips, footprint, row_block, date_slot, quality, date_gain, reprojection):
    smem = pl.BlockSpec(memory_space=pltpu.SMEM)
    return pl.pallas_call(
        bin_kernel,
        grid=(S // STEP,),
        in_specs=[
            smem,
            smem,
            smem,
            smem,
            smem,
            pl.BlockSpec((STEP * CELL, 256), lambda i: (i, 0)),
            pl.BlockSpec((256, 128), lambda i: (0, 0)),
        ],
        out_specs=pl.BlockSpec((N_TILE, TILE, 128), lambda i: (0, 0, 0)),
        out_shape=jax.ShapeDtypeStruct((N_TILE, TILE, 128), BF16),
        scratch_shapes=[
            pltpu.VMEM((N_TILE * RB, BANDS, LINES, 128), F32),
            pltpu.VMEM((N_TILE * RB, 8, 128), F32),
        ],
        name="bin_strips",
    )(footprint, row_block, date_slot, quality, date_gain, strips, reprojection)


def ring_plan(d):
    first, second = ((0, 1), (2, 3)) if d == 0 else ((2, 3), (0, 1))
    order = [(4, c) for c in first]
    for k in (3, 2, 1):
        order += [(k, c) for c in second + first]
    return first, order


def added(parts, chunk):
    total = parts[0].astype(F32)
    for part in parts[1:]:
        total = total + part.astype(F32)
    return total


def ring_kernel(
    x, comp, eto, etr, pair, sb, rv, rowf, ef, es, rh, er, psend, precv, rsend, rrecv, hsend, hrecv
):
    zone = lax.axis_index("zone")
    tile = lax.axis_index("tile")
    z = tile // 2
    core = tile - 2 * z
    other = 1 - core

    def at(dz, dt):
        return (lax.rem(zone + dz + N_ZONE, N_ZONE), lax.rem(tile + dt + N_TILE, N_TILE))

    barrier = pltpu.get_barrier_semaphore()
    friends = [(0, 1), (0, -1), (0, 2), (0, -2), (1, -1), (1, 0), (1, 1), (-1, -1), (-1, 0), (-1, 1)]
    for dz, dt in friends:
        pl.semaphore_signal(barrier, inc=1, device_id=at(dz, dt), device_id_type=MESH)
    pl.semaphore_wait(barrier, len(friends))

    partner = (zone, 2 * z + other)

    def owner(o):
        return lax.rem(z + o, NZ)

    pair_order = (4, 3, 5, 2, 6, 1, 7, 0)
    pair_copies = {}
    for o in pair_order:
        copy = pltpu.make_async_remote_copy(
            src_ref=x.at[2 * owner(o) + other],
            dst_ref=pair.at[o],
            send_sem=psend.at[o],
            recv_sem=precv.at[o],
            device_id=partner,
            device_id_type=MESH,
        )
        copy.start()
        pair_copies[o] = copy

    rowf[...] = jnp.ones_like(rowf)
    ef[...] = jnp.ones_like(ef)

    plans = [ring_plan(0), ring_plan(1)]
    have = set()
    copies = {}

    def need_pair(o):
        if o not in have:
            pair_copies[o].wait_recv()
            have.add(o)

    def gathered(o, c, arrived):
        r0, n = CHUNKS[c]
        parts = [x[2 * owner(o) + core, r0 : r0 + n, :], pair[o, r0 : r0 + n, :]]
        return added(parts + arrived, c)

    for i in range(14):
        for d in (0, 1):
            first, order = plans[d]
            k, c = order[i]
            r0, n = CHUNKS[c]
            o = k if d == 0 else (NZ - k) % NZ
            need_pair(o)
            arrived = []
            if k < 3 or (k == 3 and c in first):
                copies[d, k + 1, c].wait_recv()
                arrived = [rv[d, k, r0 : r0 + n, :]]
            total = gathered(o, c, arrived)
            if c == 0:
                both = total[0:8] + total[8:16]
                high = both.astype(BF16).astype(F32)
                sb[d, k - 1, 0:DEN, :] = jnp.concatenate([high, both - high], axis=0).astype(BF16)
                sb[d, k - 1, DEN : r0 + n, :] = total[DEN:].astype(BF16)
            else:
                sb[d, k - 1, r0 : r0 + n, :] = total.astype(BF16)
            copy = pltpu.make_async_remote_copy(
                src_ref=sb.at[d, k - 1, pl.ds(r0, n)],
                dst_ref=rv.at[d, k - 1, pl.ds(r0, n)],
                send_sem=rsend.at[d, k - 1, c],
                recv_sem=rrecv.at[d, k - 1, c],
                device_id=at(0, 2 if d == 0 else -2),
                device_id_type=MESH,
            )
            copy.start()
            copies[d, k, c] = copy

    need_pair(0)
    inverse = None
    for c in (0, 2, 1, 3):
        r0, n = CHUNKS[c]
        for d in (0, 1):
            copies[d, 1, c].wait_recv()
        total = gathered(0, c, [rv[0, 0, r0 : r0 + n, :], rv[1, 0, r0 : r0 + n, :]])
        if c == 0:
            inverse = 1.0 / jnp.maximum(total[0:8] + total[8:16], 1.0)
            total = total[DEN:]
        for h in (0, 1):
            rb = 2 * c + h
            value = total[h * CELL : (h + 1) * CELL] * inverse[rb : rb + 1]
            first_row = 16 * (LINES * rb + HALO)
            for b in range(BANDS):
                rowf[pl.ds(first_row + b, LINES, stride=16), :] = value[LINES * b : LINES * (b + 1)]
        a = 16 * c + HALO
        comp[a : a + 16] = rowf[16 * a : 16 * (a + 16), :].astype(BF16).reshape(16, 16, 128)

    which = lax.broadcasted_iota(jnp.int32, (16, 128), 0)
    lane = lax.broadcasted_iota(jnp.int32, (16, 128), 1)
    select = jnp.where(lane == jnp.where(which < 4, which, which + 120), 1.0, 0.0)
    select = jnp.where(which < 8, select, 0.0).astype(BF16)
    for b in range(BANDS):
        plane = rowf[pl.ds(b, 128, stride=16), :].astype(BF16)
        edge = lax.dot_general(select, plane, (((1,), (1,)), ((), ())), preferred_element_type=F32)
        ef[pl.ds(b, 8, stride=16), :] = edge[0:8]
    es[...] = ef[...].astype(BF16).reshape(8, 16, 128)

    sends = []

    def send(src, dst, where):
        n = len(sends)
        copy = pltpu.make_async_remote_copy(
            src_ref=src,
            dst_ref=dst,
            send_sem=hsend.at[n],
            recv_sem=hrecv.at[n],
            device_id=where,
            device_id_type=MESH,
        )
        copy.start()
        sends.append(copy)

    send(comp.at[pl.ds(HALO + ROWS - 3, 3)], rh.at[0], at(1, 0))
    send(comp.at[pl.ds(HALO, 3)], rh.at[1], at(-1, 0))
    for dz in (1, -1, 0):
        send(es.at[pl.ds(5, 3)], er.at[1 - dz], at(dz, 1))
        send(es.at[pl.ds(0, 3)], er.at[3 + 1 - dz], at(dz, -1))
    eto[...] = es[...]
    for copy in sends:
        copy.wait_recv()
    comp[0:HALO] = rh[0]
    comp[HALO + ROWS : EXT] = rh[1]
    etr[...] = er[...].reshape(18, 16, 128)
    for copy in list(pair_copies.values()) + list(copies.values()) + sends:
        copy.wait_send()


def composited(x):
    vmem = pl.BlockSpec(memory_space=pltpu.VMEM)
    dma = pltpu.SemaphoreType.DMA
    return pl.pallas_call(
        ring_kernel,
        in_specs=[vmem],
        out_specs=[vmem] * 3,
        out_shape=[
            jax.ShapeDtypeStruct((EXT, 16, 128), BF16),
            jax.ShapeDtypeStruct((8, 16, 128), BF16),
            jax.ShapeDtypeStruct((18, 16, 128), BF16),
        ],
        scratch_shapes=[
            pltpu.VMEM((NZ, TILE, 128), BF16),
            pltpu.VMEM((2, 4, TILE, 128), BF16),
            pltpu.VMEM((2, 4, TILE, 128), BF16),
            pltpu.VMEM((16 * 136, 128), F32),
            pltpu.VMEM((128, 128), F32),
            pltpu.VMEM((8, 16, 128), BF16),
            pltpu.VMEM((2, 3, 16, 128), BF16),
            pltpu.VMEM((6, 3, 16, 128), BF16),
            dma((NZ,)),
            dma((NZ,)),
            dma((2, 4, 4)),
            dma((2, 4, 4)),
            dma((8,)),
            dma((8,)),
        ],
        compiler_params=pltpu.CompilerParams(collective_id=0, has_side_effects=True),
        name="ring_composite",
    )(x)


def gelu2(v):
    inner = v * (0.7978845608028654 + 0.035677408136300125 * (v * v))
    return v + v * jnp.tanh(inner)


def pointwise(dw, x, gain, up, down):
    mean = jnp.mean(dw, axis=0, keepdims=True)
    centred = dw - mean
    var = jnp.mean(centred * centred, axis=0, keepdims=True)
    normed = (centred * lax.rsqrt(var + 1e-5) * gain).astype(BF16)
    hidden = gelu2(jnp.dot(up[...], normed, preferred_element_type=F32).astype(BF16))
    return x + jnp.dot(down[...], hidden, preferred_element_type=F32)


def column(row):
    return jnp.broadcast_to(row, (128, 128)).T


def block_kernel(
    comp, eto, etr, stem, bias, k1, g1, u1, d1, k2, g2, u2, d2, cw, cb,
    out,
    wf, w1, w1t, up1, dn1, up2, dn2, gain1, gain2, taps, cls, three, ethree, edges, hpack, feats,
):
    zone = lax.axis_index("zone")
    tile = lax.axis_index("tile")
    top, bottom = zone == 0, zone == N_ZONE - 1
    left, right = tile == 0, tile == N_TILE - 1

    bias_row = bias[...].reshape(1, 128)
    stem_f = stem[...].astype(F32)

    def stem_rows(k, tap, lanes):
        k0 = k * 16
        wf[k0 : k0 + BANDS, lanes] = stem_f * tap if tap is not None else stem_f
        b = bias_row * tap if tap is not None else bias_row
        for j in range(3):
            part = b.astype(BF16).astype(F32)
            wf[k0 + BANDS + j : k0 + BANDS + j + 1, lanes] = part
            b = b - part

    for target, swap in ((w1, False), (w1t, True)):
        wf[...] = jnp.zeros_like(wf)
        for i in range(3):
            for j in range(3):
                tap = k1[3 * i + j : 3 * i + j + 1, :].astype(F32)
                stem_rows(3 * j + i if swap else 3 * i + j, tap, slice(0, 128))
        stem_rows(4, None, slice(128, 256))
        target[...] = wf[...].T.astype(BF16)
    up1[...] = u1[...].astype(F32).T.astype(BF16)
    up2[...] = u2[...].astype(F32).T.astype(BF16)
    dn1[...] = (0.5 * d1[...].astype(F32)).T.astype(BF16)
    dn2[...] = (0.5 * d2[...].astype(F32)).T.astype(BF16)
    gain1[...] = column(g1[...].reshape(1, 128))
    gain2[...] = column(g2[...].reshape(1, 128))
    diagonal = lax.broadcasted_iota(jnp.int32, (128, 128), 0) == lax.broadcasted_iota(jnp.int32, (128, 128), 1)
    for t in range(9):
        tap = jnp.broadcast_to(k2[t : t + 1, :].astype(F32), (128, 128))
        taps[:, t * 128 : (t + 1) * 128] = jnp.where(diagonal, tap, 0.0).astype(BF16)
    wf[0:16, 0:128] = jnp.zeros((16, 128), F32)
    wf[0:11, 0:128] = cw[...].astype(F32)
    cls[...] = wf[0:16, 0:128].astype(BF16)

    def row_of(q):
        v = comp[q].astype(F32)
        if q < HALO:
            v = jnp.where(top, 0.0, v)
        if q >= HALO + ROWS:
            v = jnp.where(bottom, 0.0, v)
        return v

    lane16 = lax.broadcasted_iota(jnp.int32, (16, 128), 1)
    lane = lax.broadcasted_iota(jnp.int32, (128, 128), 1)
    low = jnp.where(top, HALO, 0)
    high = jnp.where(bottom, HALO + ROWS, EXT)
    inside16 = (lane16 >= low) & (lane16 < high)
    inside = (lane >= low) & (lane < high)

    def edge_column(side, j):
        parts = [etr[(3 * side + s) * 3 + j].astype(F32) for s in range(3)]
        before = pltpu.roll(parts[0], 64, axis=1)
        after = pltpu.roll(parts[2], 64, axis=1)
        whole = jnp.where(lane16 < HALO, before, jnp.where(lane16 < HALO + ROWS, parts[1], after))
        gone = left if side == 0 else right
        return jnp.where(inside16 & jnp.logical_not(gone), whole, 0.0)

    def own_column(k):
        v = eto[k].astype(F32)
        o = 0 if k == 0 else 127
        for q in (0, 1, 2, EXT - 3, EXT - 2, EXT - 1):
            shifted = pltpu.roll(row_of(q), (q - o) % 128, axis=1)
            v = jnp.where(lane16 == q, shifted, v)
        return jnp.where(inside16, v, 0.0)

    lefts = [edge_column(0, j) for j in range(3)] + [own_column(0)]
    rights = [own_column(7)] + [edge_column(1, j) for j in range(3)]
    for n, v in enumerate(lefts + rights):
        ethree[n, 0:16] = pltpu.roll(v, 1, axis=1).astype(BF16)
        ethree[n, 16:32] = v.astype(BF16)
        ethree[n, 32:48] = pltpu.roll(v, 127, axis=1).astype(BF16)
    before, after = lefts[2], rights[1]
    for q in range(EXT):
        v = row_of(q)
        lv = jnp.where(lane16 == 0, pltpu.roll(before, (-q) % 128, axis=1), pltpu.roll(v, 1, axis=1))
        rv = jnp.where(lane16 == 127, pltpu.roll(after, (127 - q) % 128, axis=1), pltpu.roll(v, 127, axis=1))
        three[q, 0:16] = lv.astype(BF16)
        three[q, 16:32] = v.astype(BF16)
        three[q, 32:48] = rv.astype(BF16)

    def first(parts, w):
        xs = jnp.concatenate(parts, axis=1)
        n = len(parts)
        y = jnp.dot(w[:, 0:144], xs, preferred_element_type=F32)
        gain = jnp.concatenate([gain1[...]] * n, axis=1)
        x0 = y[128:256].astype(BF16).astype(F32)
        return pointwise(y[0:128], x0, gain, up1, dn1)

    parts = [ethree[n : n + 3].reshape(144, 128) for n in (0, 1, 4, 5)]
    y = first(parts, w1t)
    for n, gone in enumerate((left, left, right, right)):
        keep = inside & jnp.logical_not(gone)
        edges[n * 128 : (n + 1) * 128] = jnp.where(keep, y[:, n * 128 : (n + 1) * 128], 0.0).astype(BF16)
    row = lax.broadcasted_iota(jnp.int32, (128, 384), 0)
    slot = lax.broadcasted_iota(jnp.int32, (128, 384), 1)
    packed = jnp.zeros((128, 384), F32)
    for n, place in enumerate((2, 3, 0, 1)):
        pick = jnp.where(slot == 4 * (row - 1) + place, 1.0, 0.0).astype(BF16)
        packed = packed + jnp.dot(edges[n * 128 : (n + 1) * 128], pick, preferred_element_type=F32)
    for g in range(3):
        hpack[g] = packed[:, g * 128 : (g + 1) * 128]

    def block1(it, carry):
        q0 = it * GROUP1
        y = first([three[pl.ds(q0 + n, 3)].reshape(144, 128) for n in range(GROUP1)], w1)
        for n in range(GROUP1):
            q = q0 + n
            v = y[:, n * 128 : (n + 1) * 128]
            out_of_grid = (top & (q < 2)) | (bottom & (q >= 2 + ROWS))
            v = jnp.where(out_of_grid, 0.0, v)
            side = pltpu.roll(hpack[q // 32], 126 - 4 * lax.rem(q, 32), axis=1)
            feats[q, 0] = jnp.where(lane < 2, side, pltpu.roll(v, 2, axis=1)).astype(BF16)
            feats[q, 1] = v.astype(BF16)
            feats[q, 2] = jnp.where(lane >= 126, side, pltpu.roll(v, 126, axis=1)).astype(BF16)
        return carry

    lax.fori_loop(0, MID // GROUP1, block1, 0)

    k16 = lax.broadcasted_iota(jnp.int32, (16, 128 * GROUP2), 0)
    cbias = jnp.full((16, 128 * GROUP2), -1e30, F32)
    for k in range(11):
        cbias = jnp.where(k16 == k, cb[k], cbias)

    def block2(it, carry):
        q0 = it * GROUP2
        around = []
        for i in range(3):
            for j in range(3):
                around.append(jnp.concatenate([feats[q0 + n + 2 * i, j] for n in range(GROUP2)], axis=1))
        dw = jnp.dot(taps[...], jnp.concatenate(around, axis=0), preferred_element_type=F32)
        x = jnp.concatenate([feats[q0 + 2 + n, 1] for n in range(GROUP2)], axis=1).astype(F32)
        gain = jnp.concatenate([gain2[...]] * GROUP2, axis=1)
        y = pointwise(dw, x, gain, up2, dn2).astype(BF16)
        logits = jnp.dot(cls[...], y, preferred_element_type=F32) + cbias
        e = jnp.exp(logits - jnp.max(logits, axis=0, keepdims=True))
        probs = e / jnp.sum(e, axis=0, keepdims=True)
        for n in range(GROUP2):
            out[pl.ds(q0 + n, 11, stride=ROWS), :] = probs[0:11, n * 128 : (n + 1) * 128]
        return carry

    lax.fori_loop(0, ROWS // GROUP2, block2, 0)


def classified(comp, eto, etr, *weights):
    vmem = pl.BlockSpec(memory_space=pltpu.VMEM)
    return pl.pallas_call(
        block_kernel,
        in_specs=[vmem] * 14 + [pl.BlockSpec(memory_space=pltpu.SMEM)],
        out_specs=vmem,
        out_shape=jax.ShapeDtypeStruct((11 * ROWS, 128), F32),
        scratch_shapes=[
            pltpu.VMEM((256, 256), F32),
            pltpu.VMEM((256, 256), BF16),
            pltpu.VMEM((256, 256), BF16),
            pltpu.VMEM((512, 128), BF16),
            pltpu.VMEM((128, 512), BF16),
            pltpu.VMEM((512, 128), BF16),
            pltpu.VMEM((128, 512), BF16),
            pltpu.VMEM((128, 128), F32),
            pltpu.VMEM((128, 128), F32),
            pltpu.VMEM((128, 9 * 128), BF16),
            pltpu.VMEM((16, 128), BF16),
            pltpu.VMEM((EXT, 48, 128), BF16),
            pltpu.VMEM((8, 48, 128), BF16),
            pltpu.VMEM((512, 128), BF16),
            pltpu.VMEM((3, 128, 128), F32),
            pltpu.VMEM((MID, 3, 128, 128), BF16),
        ],
        name="blocks",
    )(comp, eto, etr, *weights)


def shards(
    strips,
    footprint,
    row_block,
    date_slot,
    quality,
    date_gain,
    reprojection,
    stem_weight,
    stem_bias,
    depth_near,
    gain_near,
    up_near,
    down_near,
    depth_far,
    gain_far,
    up_far,
    down_far,
    class_weight,
    class_bias,
):
    rows = jnp.transpose(strips, (0, 2, 1, 3)).reshape(S * CELL, 256)
    x = binned(rows, footprint.reshape(S), row_block, date_slot, quality, date_gain, reprojection)
    comp, eto, etr = composited(x)
    probs = classified(
        comp,
        eto,
        etr,
        stem_weight,
        stem_bias,
        depth_near,
        gain_near,
        up_near,
        down_near,
        depth_far,
        gain_far,
        up_far,
        down_far,
        class_weight.T,
        class_bias,
    )
    return jnp.transpose(probs.reshape(11, ROWS, 128), (1, 0, 2))


def solution(mesh):
    each = P(("zone", "tile"))
    in_specs = (
        P(("zone", "tile"), None, None, None),
        P(("zone", "tile"), None),
        each,
        each,
        each,
    ) + (P(),) * 14
    return jax.shard_map(
        shards, mesh=mesh, in_specs=in_specs, out_specs=P("zone", None, "tile"), check_vma=False
    )
```

time: 311 us -> 79.8 us (0.26); the launches traced: 307 us -> 79.6 us
  waiting for transfers between devices: 145 us -> 0 us
  Pallas kernels: 0 us -> 79.6 us
  matrix products: 52.3 us -> 0 us
  starting transfers between devices: 37.9 us -> 0 us
  other arithmetic: 32.5 us -> 0 us
  local copies, waits for them, and re-layouts: 29.1 us -> 0 us
  loops' own time: 9.68 us -> 0 us
    all_to_all x2 -> x0, waiting for transfers between devices: 131 us -> none  [the longest x1 131 us: shards(): lax.all_to_all(outgoing, 'tile', split_axis=0, concat_axis=0, tiled=True)]
    pallas_call x0 -> x3, Pallas kernels: none -> 79.6 us  [the longest x1 37.9 us: composited(): pl.pallas_call(ring_kernel, in_specs=[vmem], out_specs=[vmem] * 3, out_sh...]
    dot_general x18 -> x0, matrix products: 50.1 us -> none  [the longest x16 44.1 us: one_block(): jnp.einsum('rho,hc->rco', hidden, down, preferred_element_type=jnp.float32)]
    ppermute x8 -> x0, starting transfers between devices: 20.7 us -> none  [the longest x4 14.1 us: padded_2(): before = lax.ppermute(last, axis, up)]
    reduce_sum x35 -> x0, other arithmetic: 20.2 us -> none  [the longest x16 12.7 us: one_block(): average = jnp.mean(total, axis=1, keepdims=True)]
    all_to_all x2 -> x0, starting transfers between devices: 17.2 us -> none  [the longest x1 9.98 us: shards(): lax.all_to_all(placed, 'tile', split_axis=0, concat_axis=0, tiled=True)]
    ppermute x8 -> x0, waiting for transfers between devices: 13.4 us -> none  [the longest x4 13.4 us: padded_2(): after = lax.ppermute(leading, axis, down)]
    another operation x2 -> x0, loops' own time: 9.68 us -> none  [convnext(): pieces = lax.map(one_block, jnp.arange(rows // 8, dtype=jnp.int32))]
  transfers between devices with their start and end apart: 10 -> 0, of which waited for: 5 -> 0; matrix products, arithmetic and copies ran while one was open for 4% -> 0% of each run, Pallas kernels for 0% -> 0%
where the time goes in v1:
time: 79.8 us; the launch traced here: 79.6 us
  Pallas kernels  79.6 us (100%)
    pallas_call x1, Pallas kernels, composited(): pl.pallas_call(ring_kernel, in_specs=[vmem], out_specs=[vmem] * 3, out_sh...  37.9 us
    pallas_call x1, Pallas kernels, classified(): pl.pallas_call(block_kernel, in_specs=[vmem] * 14 + [pl.BlockSpec(memory_...  34.4 us
    pallas_call x1, Pallas kernels, binned(): pl.pallas_call(bin_kernel, grid=(S // STEP,), in_specs=[smem, smem, smem,...  7.28 us

profile of v1, /device:TPU:1, one launch (start us, length us, event | category | flops | bytes accessed | tf_op | source)
XLA Modules:
  0.0 79.6 jit_solution(1953182389048106530)
XLA Ops:
  0.0 7.3 %bin_strips.1.x = bf16[16,848,128]{2,1,0:T(8,128)(2,1)} custom-call(s32[48]{0:T(128)} %bitcast.10, s32[48]{0:T(128)} %rb.1, s32[48]{0:T(128)} %ds.1, s32[48]{0:T(128)} %q.1, f32[12]{0:T(128)} %dg.1, bf16[4992,256]{1,0:T(8,128)(2,1)} %bitcast.8, bf16[256,128]{1,0:T(8,128)(2,1)} %reproj.1), custom_call_target="tpu_custom_call" | custom-call | tf_op jit(solution)/shard_map/bin_strips/pallas_call | solution.py:72
  7.3 37.9 %ring_composite.1 = (bf16[70,16,128]{2,1,0:T(8,128)(2,1)}, bf16[8,16,128]{2,1,0:T(8,128)(2,1)}, bf16[18,16,128]{2,1,0:T(8,128)(2,1)}) custom-call(bf16[16,848,128]{2,1,0:T(8,128)(2,1)} %bin_strips.1.x), custom_call_target="tpu_custom_call" | custom-call | tf_op jit(solution)/shard_map/ring_composite/pallas_call | solution.py:255
  45.2 34.4 %blocks.1 = f32[704,128]{1,0:T(8,128)} custom-call(bf16[70,16,128]{2,1,0:T(8,128)(2,1)} %get-tuple-element.8.comp, bf16[8,16,128]{2,1,0:T(8,128)(2,1)} %get-tuple-element.9.eto, bf16[18,16,128]{2,1,0:T(8,128)(2,1)} %get-tuple-element.10.etr, bf16[13,128]{1,0:T(8,128)(2,1)} %stem.1, f32[128]{0:T(128)} %bias.1, bf16[9,128]{1,0:T(8,128)(2,1)} %k1.1, f32[128]{0:T(128)} %g1.1, ...), custom_call_target="tpu_custom_call" | custom-call | tf_op jit(solution)/shard_map/blocks/pallas_call | solution.py:458
